TPU v7x, 32 devices: a whole 2x2x4 slice. The times are simulated.
32 devices in a mesh: ens: 2 (over y), grid: 16 (over z, x, core).
Axes of the slice: x: 2, y: 2, z: 4, core: 2. Of those that a mesh axis runs over, the one named last changes fastest.
Arguments:
- fields: bfloat16 [2, 384, 768, 256], P('ens', 'grid'), may hold values from -6 to 6
- mode_counts: int32 [384], P('grid'), may hold values from 96 to 384, as said below
- gain_attn: float32 [256], replicated, may hold values from 0.5 to 1.5
- w_query: bfloat16 [256, 256], replicated, may hold values from -1 to 1
- w_key: bfloat16 [256, 256], replicated, may hold values from -8 to 8
- w_value: bfloat16 [256, 256], replicated, may hold values from -0.375 to 0.375
- w_out: bfloat16 [256, 256], replicated, may hold values from -0.375 to 0.375
- gain_spec: float32 [256], replicated, may hold values from 0.5 to 1.5
- w_first: bfloat16 [2, 8, 32, 32], replicated, may hold values from -1 to 1
- w_second: bfloat16 [2, 8, 32, 32], replicated, may hold values from -1 to 1
Outputs:
- layer_out: bfloat16 [2, 384, 768, 256], P('ens', 'grid')
Inputs may be any that keep to these rules, and one draw needn't show every extreme that they name: `mode_counts`: longitude wavenumbers kept in each latitude row; some row keeps all 384.
All inputs are finite; a program needn't handle non-finite values.
Results may differ from a plain program's by a relative error of at most 0.012.
Values may be sent and summed in bfloat16 or wider, within the bound.
A program may use at most 256 MiB of HBM per device.

v0:
```python
import math
import jax
import jax.numpy as jnp
from jax import lax
from jax.sharding import PartitionSpec as P

HEAD = 32
NLAT = 384
KLON = 384
KLAT = 128
norm_eps = 1e-05


def layer_norm(inputs, gain_vec):
    widened = inputs.astype(jnp.float32)
    center = widened - jnp.mean(widened, axis=-1, keepdims=True)
    spread = jnp.mean(center * center, axis=-1, keepdims=True)
    return center * lax.rsqrt(spread + norm_eps) * gain_vec


def lon_table(points, mode_count):
    positions = jnp.arange(points, dtype=jnp.int32)
    frequency = jnp.arange(mode_count, dtype=jnp.int32)
    turn_count = positions[:, None] * frequency[None, :] % points
    angles = 2.0 * math.pi / points * turn_count.astype(jnp.float32)
    factor = 1.0 / math.sqrt(points)
    return jnp.concatenate([jnp.cos(angles) * factor, -jnp.sin(angles) * factor], axis=1).astype(
        jnp.bfloat16
    )


def lon_inverse(points, mode_count):
    positions = jnp.arange(points, dtype=jnp.int32)
    frequency = jnp.arange(mode_count, dtype=jnp.int32)
    turn_count = frequency[:, None] * positions[None, :] % points
    angles = 2.0 * math.pi / points * turn_count.astype(jnp.float32)
    weight = jnp.where(frequency == 0, 1.0, 2.0).astype(jnp.float32)[:, None] / math.sqrt(points)
    return jnp.stack([jnp.cos(angles) * weight, -jnp.sin(angles) * weight]).astype(jnp.bfloat16)


def lat_angles(row_count, mode_count):
    frequency = jnp.arange(mode_count, dtype=jnp.int32)
    frequency = jnp.where(frequency < mode_count // 2, frequency, frequency - mode_count)
    positions = jnp.arange(row_count, dtype=jnp.int32)
    turn_count = frequency[:, None] * positions[None, :] % row_count
    return 2.0 * math.pi / row_count * turn_count.astype(jnp.float32)


def lat_forward(row_count, mode_count):
    angles = lat_angles(row_count, mode_count)
    factor = 1.0 / math.sqrt(row_count)
    cosine = jnp.cos(angles) * factor
    sine_part = jnp.sin(angles) * factor
    return jnp.stack(
        [jnp.stack([cosine, sine_part], axis=1), jnp.stack([-sine_part, cosine], axis=1)]
    ).astype(jnp.bfloat16)


def lat_inverse(row_count, mode_count):
    angles = jnp.transpose(lat_angles(row_count, mode_count))
    factor = 1.0 / math.sqrt(row_count)
    cosine = jnp.cos(angles) * factor
    sine_part = jnp.sin(angles) * factor
    return jnp.stack([jnp.stack([cosine, -sine_part]), jnp.stack([sine_part, cosine])]).astype(
        jnp.bfloat16
    )


def complex_blocks(weight):
    real_part = weight[0]
    imag_part = weight[1]
    return jnp.stack([jnp.stack([real_part, imag_part]), jnp.stack([-imag_part, real_part])])


def mix_blocks(spec, big):
    blocks = spec.reshape(spec.shape[:4] + (big.shape[2], big.shape[3]))
    out_blocks = jnp.einsum("mpqkbi,psbio->msqkbo", blocks, big, preferred_element_type=jnp.float32)
    return out_blocks.reshape(spec.shape)


def mix_members(all_scores, all_values, head_count):
    members, lat_rows, lon_points, feat_dim = all_values.shape
    row_max = jnp.max(all_scores, axis=0, keepdims=True)
    exps = jnp.exp(all_scores - row_max)
    totals = jnp.sum(exps, axis=0)
    weights = exps.astype(jnp.bfloat16)
    split_values = all_values.reshape(members, lat_rows, lon_points, head_count, HEAD)
    mixed_out = jnp.einsum(
        "nmlhw,nlwhe->mlwhe", weights, split_values, preferred_element_type=jnp.float32
    )
    mixed_out = mixed_out / jnp.transpose(totals, (0, 1, 3, 2))[..., None]
    return mixed_out.astype(jnp.bfloat16).reshape(
        all_scores.shape[1], lat_rows, lon_points, feat_dim
    )


def shards(
    fields, mode_counts, gain_attn, w_query, w_key, w_value, w_out, gain_spec, w_first, w_second
):
    mem_dev, lat_dev, lon_points, feat_dim = fields.shape
    head_count = feat_dim // HEAD
    score_scale = 1.0 / math.sqrt(HEAD)
    normed = layer_norm(fields, gain_attn).astype(jnp.bfloat16)
    queries = jnp.dot(normed, w_query, preferred_element_type=jnp.float32).astype(jnp.bfloat16)
    queries = queries.reshape(mem_dev, lat_dev, lon_points, head_count, HEAD)
    own_keys = jnp.dot(normed, w_key, preferred_element_type=jnp.float32).astype(jnp.bfloat16)
    own_values = jnp.dot(normed, w_value, preferred_element_type=jnp.float32).astype(jnp.bfloat16)
    key_rows = lax.all_gather(own_keys, "ens", axis=0, tiled=True)
    split_keys = key_rows.reshape(key_rows.shape[:3] + (head_count, HEAD))
    scores = (
        jnp.einsum("mlwhe,nlwhe->nmlhw", queries, split_keys, preferred_element_type=jnp.float32)
        * score_scale
    )
    all_values = lax.all_gather(own_values, "ens", axis=0, tiled=True)
    mixed_out = mix_members(scores, all_values, head_count)
    attended = (
        fields.astype(jnp.float32) + jnp.dot(mixed_out, w_out, preferred_element_type=jnp.float32)
    ).astype(jnp.bfloat16)
    retained = (jnp.arange(KLON, dtype=jnp.int32)[None, :] < mode_counts[:, None]).astype(
        jnp.float32
    )
    normed_two = layer_norm(attended, gain_spec).astype(jnp.bfloat16)
    spectrum = jnp.einsum(
        "mlxd,xk->mlkd", normed_two, lon_table(lon_points, KLON), preferred_element_type=jnp.float32
    )
    spectrum = spectrum.reshape(mem_dev, lat_dev, 2, KLON, feat_dim)
    spectrum = (spectrum * retained[None, :, None, :, None]).astype(jnp.bfloat16)
    forward = lat_forward(NLAT, KLAT)
    inverse = lat_inverse(NLAT, KLAT)
    big_one = complex_blocks(w_first)
    big_two = complex_blocks(w_second)
    rows_spec = jnp.einsum(
        "pqrj,mjrkd->mpqkd",
        forward,
        lax.all_to_all(spectrum, "grid", split_axis=3, concat_axis=1, tiled=True),
        preferred_element_type=jnp.float32,
    ).astype(jnp.bfloat16)
    hidden = jnp.maximum(mix_blocks(rows_spec, big_one), 0.0).astype(jnp.bfloat16)
    second = mix_blocks(hidden, big_two).astype(jnp.bfloat16)
    back_rows = jnp.einsum(
        "rpjq,mpqkd->mjrkd", inverse, second, preferred_element_type=jnp.float32
    ).astype(jnp.bfloat16)
    returned = lax.all_to_all(back_rows, "grid", split_axis=1, concat_axis=3, tiled=True)
    returned = returned * retained.astype(jnp.bfloat16)[None, :, None, :, None]
    field_out = jnp.einsum(
        "mjrkd,rkx->mjxd",
        returned,
        lon_inverse(lon_points, KLON),
        preferred_element_type=jnp.float32,
    )
    return (attended.astype(jnp.float32) + field_out).astype(jnp.bfloat16)


def solution(mesh):
    in_specs = (P("ens", "grid", None, None), P("grid"), P(), P(), P(), P(), P(), P(), P(), P())
    out_specs = P("ens", "grid", None, None)
    return jax.shard_map(shards, mesh=mesh, in_specs=in_specs, out_specs=out_specs, check_vma=False)
```

profile of v0, /device:TPU:11, one launch (start us, length us, event | category | flops | bytes accessed | tf_op | source)
XLA Modules:
  0.0 1163.1 jit_solution(6597510635387888419)
XLA Ops:
  6.5 12.6 %copy.142 = bf16[1,24,768,256]{2,3,1,0:T(8,128)(2,1)} copy(bf16[1,24,768,256]{3,2,1,0:T(8,128)(2,1)} %param.10) | data formatting | bytes 18874368 | tf_op args[0]
  28.2 11.0 convolution_convert_fusion.1
  40.1 13.7 %convolution_convert_fusion.2 = bf16[24,768,256]{2,1,0:T(8,128)(2,1)} fusion(bf16[256,256]{1,0:T(8,128)(2,1)S(1)} %copy-done.11, bf16[1,24,768,256]{2,3,1,0:T(8,128)(2,1)} %copy.142, f32[256]{0:T(256)S(1)} %copy-done.8, f32[24,768]{1,0:T(8,128)S(1)} %add_rsqrt_fusion.1, f32[24,768]{1,0:T(8,128)S(1)} %broadcast_multiply_fusion.1), kind=kOutput, calls=%fused_computation.36 | convolution fusion | flops 2444230656 | bytes 19153920 | tf_op jit(solution)/shard_map/dot_general | solution.py:107
  59.8 15.2 %bitcast_convert_fusion.3 = f32[24,8,768,32]{2,3,1,0:T(8,128)} fusion(bf16[256,256]{1,0:T(8,128)(2,1)S(1)} %copy-done.4, bf16[1,24,768,256]{2,3,1,0:T(8,128)(2,1)} %copy.142, f32[256]{0:T(256)S(1)} %copy-done.8, f32[24,768]{1,0:T(8,128)S(1)} %add_rsqrt_fusion.1, f32[24,768]{1,0:T(8,128)S(1)} %broadcast_multiply_fusion.1), kind=kOutput, calls=%fused_computation.143 | convolution fusion | flops 2448949248 | bytes 28591104 | tf_op jit(solution)/shard_map/dot_general | solution.py:104
  75.0 189.7 %all-gather.7.cloned.1.call-done = bf16[48,768,256]{2,1,0:T(8,128)(2,1)} async-done(((bf16[24,768,256]{2,1,0:T(8,128)(2,1)}), bf16[48,768,256]{2,1,0:T(8,128)(2,1)}) %all-gather.7.cloned.1.call-update) | async-done | bytes 18874384 | tf_op jit(solution)/shard_map/all_gather | solution.py:108
  264.7 24.2 %copy.207 = bf16[48,768,256]{1,2,0:T(8,128)(2,1)} copy(bf16[48,768,256]{2,1,0:T(8,128)(2,1)} %all-gather.7.cloned.1.call-done) | data formatting | bytes 37748736
  288.9 17.8 %multiply_reduce_fusion.1 = f32[24,8,768,2]{2,1,0,3:T(8,128)S(1)} fusion(bf16[24,8,768,32,2]{2,3,1,0,4:T(8,128)(2,1)} %bitcast.170, f32[24,8,768,32]{2,3,1,0:T(8,128)} %bitcast_convert_fusion.3), kind=kLoop, calls=%fused_computation.1 | loop fusion | flops 28016640 | bytes 38928384
  307.1 183.5 %all-gather.5.cloned.1.call-done = bf16[48,768,256]{2,1,0:T(8,128)(2,1)} async-done(((bf16[24,768,256]{2,1,0:T(8,128)(2,1)}), bf16[48,768,256]{2,1,0:T(8,128)(2,1)}) %all-gather.5.cloned.1.call-update) | async-done | bytes 18874384 | tf_op jit(solution)/shard_map/all_gather | solution.py:114
  490.6 24.6 %copy.206 = bf16[48,768,256]{1,2,0:T(8,128)(2,1)} copy(bf16[48,768,256]{2,1,0:T(8,128)(2,1)} %all-gather.5.cloned.1.call-done) | data formatting | bytes 37748736
  515.2 13.5 %multiply_reduce_fusion = f32[24,768,8,32]{1,3,2,0:T(8,128)S(1)} fusion(bf16[24,768,8,2,32]{1,4,2,0,3:T(8,128)(2,1)} %bitcast.171, f32[24,768,8,2]{1,2,3,0:T(8,128)S(1)} %get-tuple-element.6), kind=kLoop, calls=%fused_computation | loop fusion | flops 23592960 | bytes 38928384 | tf_op jit(solution)/shard_map/nmlhw,nlwhe->mlwhe/dot_general | solution.py:88
  533.6 20.6 %convert_reduce_fusion = (f32[24,768]{1,0:T(8,128)S(1)}, bf16[1,24,768,256]{2,3,1,0:T(8,128)(2,1)}) fusion(bf16[24,768,256]{1,2,0:T(8,128)(2,1)} %bitcast.172, bf16[256,256]{1,0:T(8,128)(2,1)S(1)} %copy-done, bf16[1,24,768,256]{2,3,1,0:T(8,128)(2,1)} %copy.142), kind=kOutput, calls=%fused_computation.4 | convolution fusion | flops 2439493632 | bytes 28516352 | tf_op jit(solution)/shard_map/dot_general | solution.py:117
  560.6 10.8 fusion.15
  571.4 7.6 multiply_convert_fusion
  579.0 39.1 %copy.160 = bf16[1,24,2,384,256]{4,2,1,0,3:T(2,128)(2,1)} copy(bf16[1,24,2,384,256]{4,3,2,1,0:T(8,128)(2,1)S(1)} %multiply_convert_fusion) | data formatting | bytes 18874368 | tf_op jit(solution)/shard_map/convert_element_type | solution.py:127
  627.0 202.5 %all-to-all-done = bf16[1,24,2,384,256]{4,2,1,0,3:T(2,128)(2,1)} async-done(((bf16[1,24,2,384,256]{4,2,1,0,3:T(2,128)(2,1)}), bf16[1,24,2,384,256]{4,2,1,0,3:T(2,128)(2,1)}, u32[]{:S(2)}, u32[]{:S(2)}) %all-to-all-start) | async-done | bytes 9437216 | tf_op jit(solution)/shard_map/all_to_all | solution.py:135
  829.6 10.7 copy.161
  840.3 8.3 copy.162
  848.6 19.5 %bitcast_convert_fusion.2 = bf16[24,256,2,128]{3,1,2,0:T(8,128)(2,1)S(1)} fusion(bf16[384,2,24,256,1]{3,2,1,0,4:T(8,128)(2,1)} %bitcast.178, bf16[1,128,2,384]{3,1,2,0:T(8,128)(2,1)S(1)} %get-tuple-element.14, bf16[1,128,2,384]{3,1,2,0:T(8,128)(2,1)S(1)} %get-tuple-element.13), kind=kOutput, calls=%fused_computation.40 | convolution fusion | flops 2418278400 | bytes 12976128 | tf_op jit(solution)/shard_map/pqrj,mjrkd->mpqkd/dot_general | solution.py:132
  876.4 24.0 %copy.168 = bf16[1,384,2,24,256]{4,2,3,0,1:T(2,128)(2,1)} copy(bf16[1,384,2,24,256]{1,4,2,3,0:T(8,128)(2,1)} %fusion.12) | data formatting | bytes 18874368 | tf_op jit(solution)/shard_map/convert_element_type | solution.py:142
  910.6 199.5 %all-to-all-done.1 = bf16[1,384,2,24,256]{4,2,3,0,1:T(2,128)(2,1)} async-done(((bf16[1,384,2,24,256]{4,2,3,0,1:T(2,128)(2,1)}), bf16[1,384,2,24,256]{4,2,3,0,1:T(2,128)(2,1)}, u32[]{:S(2)}, u32[]{:S(2)}) %all-to-all-start.1) | async-done | bytes 9437216 | tf_op jit(solution)/shard_map/all_to_all | solution.py:143
  1110.2 8.9 copy.169
  1119.1 8.6 copy.170
  1127.7 15.6 %fusion.11 = bf16[1,24,768,256]{2,3,1,0:T(8,128)(2,1)} fusion(bf16[1,24,768,256]{2,3,1,0:T(8,128)(2,1)} %get-tuple-element.26, bf16[24,2,384,256]{3,2,1,0:T(8,128)(2,1)} %bitcast.177, bf16[24,384]{1,0:T(8,128)(2,1)S(1)} %copy-done.7, bf16[1,384,768]{1,2,0:T(8,128)(2,1)S(1)} %get-tuple-element.16, bf16[1,384,768]{1,2,0:T(8,128)(2,1)S(1)} %get-tuple-element.15), kind=kOutput, calls=%fused_computation.19 | convolution fusion | flops 7283146752 | bytes 29509632 | tf_op jit(solution)/shard_map/mjrkd,rkx->mjxd/dot_general | solution.py:145
  1143.3 12.6 %copy.172 = bf16[1,24,768,256]{3,2,1,0:T(8,128)(2,1)} copy(bf16[1,24,768,256]{2,3,1,0:T(8,128)(2,1)} %fusion.11) | data formatting | bytes 18874368 | tf_op jit(solution)/shard_map/convert_element_type | solution.py:151
  (61 shorter events, 54.8 us)
Async XLA Ops:
  6.5 527.0 %copy-start = (bf16[256,256]{1,0:T(8,128)(2,1)S(1)}, bf16[256,256]{1,0:T(8,128)(2,1)}, u32[]{:S(2)}) copy-start(bf16[256,256]{1,0:T(8,128)(2,1)} %param.16) | copy-start | bytes 393220
  6.5 258.1 %all-gather.7.cloned.1.call-start = ((), (), s32[]{:S(2)}) async-start(), calls=%async_computation.3 | async-start | bytes 28311552 | tf_op jit(solution)/shard_map/all_gather | solution.py:108
  19.2 6.4 copy-start.2
  19.2 9.0 copy-start.8
  19.2 9.0 copy-start.10
  39.2 0.9 copy-start.11
  39.2 451.4 %all-gather.5.cloned.1.call-start = ((), (), s32[]{:S(2)}) async-start(), calls=%async_computation.2 | async-start | bytes 28311552 | tf_op jit(solution)/shard_map/all_gather | solution.py:114
  53.8 5.3 copy-start.9
  53.8 6.0 copy-start.4
  554.2 6.5 copy-start.3
  554.2 6.5 copy-start.12
  618.1 6.6 copy-start.5
  618.1 6.8 copy-start.6
  618.1 211.5 %all-to-all-start = ((bf16[1,24,2,384,256]{4,2,1,0,3:T(2,128)(2,1)}), bf16[1,24,2,384,256]{4,2,1,0,3:T(2,128)(2,1)}, u32[]{:S(2)}, u32[]{:S(2)}) async-start(bf16[1,24,2,384,256]{4,2,1,0,3:T(2,128)(2,1)} %copy.160), calls=%async_computation | async-start | bytes 18874368 | tf_op jit(solution)/shard_map/all_to_all | solution.py:135
  900.3 209.9 %all-to-all-start.1 = ((bf16[1,384,2,24,256]{4,2,3,0,1:T(2,128)(2,1)}), bf16[1,384,2,24,256]{4,2,3,0,1:T(2,128)(2,1)}, u32[]{:S(2)}, u32[]{:S(2)}) async-start(bf16[1,384,2,24,256]{4,2,3,0,1:T(2,128)(2,1)} %copy.168), calls=%async_computation.1 | async-start | bytes 18874368 | tf_op jit(solution)/shard_map/all_to_all | solution.py:143
  1119.1 8.6 copy-start.7
  1127.7 28.1 %copy-start.1 = (bf16[256,256]{1,0:T(8,128)(2,1)S(1)}, bf16[256,256]{1,0:T(8,128)(2,1)}, u32[]{:S(2)}) copy-start(bf16[256,256]{1,0:T(8,128)(2,1)} %param.16) | copy-start | bytes 393220
Sparse Core Ops, SparseCore 0:
  39.3 225.2 all-gather.6
  266.2 224.3 all-gather.4
where the time goes:
time: 1170 us; the launch traced here: 1160 us
  waiting for transfers between devices  775 us (66%)
  local copies, waits for them, and re-layouts  177 us (15%)
  matrix products  114 us (10%)
  other arithmetic  71.3 us (6%)
  between operations  14.1 us (1%)
  starting transfers between devices  11.8 us (1%)
    all_to_all x1, waiting for transfers between devices, shards(): lax.all_to_all(spectrum, 'grid', split_axis=3, concat_axis=1, tiled=True)  203 us
    all_to_all x1, waiting for transfers between devices, shards(): lax.all_to_all(back_rows, 'grid', split_axis=1, concat_axis=3, tiled=True)  200 us
    all_gather x1, waiting for transfers between devices, shards(): key_rows = lax.all_gather(own_keys, 'ens', axis=0, tiled=True)  190 us
    all_gather x1, waiting for transfers between devices, shards(): all_values = lax.all_gather(own_values, 'ens', axis=0, tiled=True)  184 us
    unnamed x31, local copies, waits for them, and re-layouts  63.8 us
    convert_element_type x1, local copies, waits for them, and re-layouts, shards(): (spectrum * retained[None, :, None, :, None]).astype(jnp.bfloat16)  39.1 us
    convert_element_type x1, local copies, waits for them, and re-layouts, shards(): back_rows = jnp.einsum('rpjq,mpqkd->mjrkd', inverse, second, preferred_el...  24 us
  transfers between devices with their start and end apart: 4, of which 4 were waited for; matrix products, arithmetic and copies ran while one was open for 7% of the time, Pallas kernels for 0%

commit v1 on v0

--- a/solution.py
+++ b/solution.py
@@ -111,7 +111,8 @@
         jnp.einsum("mlwhe,nlwhe->nmlhw", queries, split_keys, preferred_element_type=jnp.float32)
         * score_scale
     )
-    all_values = lax.all_gather(own_values, "ens", axis=0, tiled=True)
+    repeated = jnp.stack([own_values] * lax.axis_size("ens"))
+    all_values = jnp.concatenate(lax.all_to_all(repeated, "ens", 0, 0), axis=0)
     mixed_out = mix_members(scores, all_values, head_count)
     attended = (
         fields.astype(jnp.float32) + jnp.dot(mixed_out, w_out, preferred_element_type=jnp.float32)

time: 1170 us -> 1200 us (1.026)
  other arithmetic: 71.3 us -> 99.3 us
    all_to_all x0 -> x1, waiting for transfers between devices: none -> 366 us  [shards(): all_values = jnp.concatenate(lax.all_to_all(repeated, 'ens', 0, 0), axis=0)]
    all_gather x1, waiting for transfers between devices: 190 us -> 0.01 us  [shards(): key_rows = lax.all_gather(own_keys, 'ens', axis=0, tiled=True)]
    all_gather x1 -> x0, waiting for transfers between devices: 184 us -> none  [shards(): all_values = lax.all_gather(own_values, 'ens', axis=0, tiled=True)]
    another operation x4 -> x5, other arithmetic: 12.2 us -> 29.7 us  [the longest x1 17.8 us: shards(): repeated = jnp.stack([own_values] * lax.axis_size('ens'))]
    unnamed x31 -> x41, local copies, waits for them, and re-layouts: 63.8 us -> 64.2 us
  transfers between devices with their start and end apart: 4 -> 4, of which waited for: 4 -> 3; matrix products, arithmetic and copies ran while one was open for 7% -> 7% of each run, Pallas kernels for 0% -> 0%
where the time goes in v1:
time: 1200 us; the launch traced here: 1190 us
  waiting for transfers between devices  768 us (64%)
  local copies, waits for them, and re-layouts  177 us (15%)
  matrix products  111 us (9%)
  other arithmetic  99.3 us (8%)
  starting transfers between devices  22.5 us (2%)
  between operations  14.2 us (1%)
    all_to_all x1, waiting for transfers between devices, shards(): all_values = jnp.concatenate(lax.all_to_all(repeated, 'ens', 0, 0), axis=0)  366 us
    all_to_all x1, waiting for transfers between devices, shards(): lax.all_to_all(spectrum, 'grid', split_axis=3, concat_axis=1, tiled=True)  203 us
    all_to_all x1, waiting for transfers between devices, shards(): lax.all_to_all(back_rows, 'grid', split_axis=1, concat_axis=3, tiled=True)  200 us
    unnamed x41, local copies, waits for them, and re-layouts  64.2 us
    convert_element_type x1, local copies, waits for them, and re-layouts, shards(): (spectrum * retained[None, :, None, :, None]).astype(jnp.bfloat16)  39.1 us
  transfers between devices with their start and end apart: 4, of which 3 were waited for; matrix products, arithmetic and copies ran while one was open for 7% of the time, Pallas kernels for 0%

profile of v1, /device:TPU:11, one launch (start us, length us, event | category | flops | bytes accessed | tf_op | source)
XLA Modules:
  0.0 1192.5 jit_solution(2181211197678035927)
XLA Ops:
  6.5 12.6 %copy.142 = bf16[1,24,768,256]{2,3,1,0:T(8,128)(2,1)} copy(bf16[1,24,768,256]{3,2,1,0:T(8,128)(2,1)} %param.10) | data formatting | bytes 18874368 | tf_op args[0]
  28.2 11.1 convolution_convert_fusion.1
  40.2 13.7 %convert_bitcast_fusion = bf16[1,1,24,768,256]{4,3,2,1,0:T(8,128)(2,1)} fusion(bf16[256,256]{1,0:T(8,128)(2,1)S(1)} %copy-done.11, bf16[1,24,768,256]{2,3,1,0:T(8,128)(2,1)} %copy.142, f32[256]{0:T(256)S(1)} %copy-done.8, f32[24,768]{1,0:T(8,128)S(1)} %add_rsqrt_fusion.1, f32[24,768]{1,0:T(8,128)S(1)} %broadcast_multiply_fusion.1), kind=kOutput, calls=%fused_computation.35 | convolution fusion | flops 2444230656 | bytes 19153920 | tf_op jit(solution)/shard_map/dot_general | solution.py:107
  53.8 17.8 %pad_maximum_fusion = bf16[2,1,24,768,256]{4,3,2,1,0:T(8,128)(2,1)} fusion(bf16[1,1,24,768,256]{4,3,2,1,0:T(8,128)(2,1)} %convert_bitcast_fusion), kind=kLoop, calls=%fused_computation.20 | loop fusion | flops 9437184 | bytes 28311552 | tf_op jit(solution)/shard_map/stack | solution.py:114
  71.7 10.9 all-to-all-start
  88.3 13.2 %bitcast_convert_fusion.3 = f32[24,8,768,32]{2,3,1,0:T(8,128)} fusion(bf16[256,256]{1,0:T(8,128)(2,1)S(1)} %copy-done.4, bf16[1,24,768,256]{2,3,1,0:T(8,128)(2,1)} %copy.142, f32[256]{0:T(256)S(1)} %copy-done.8, f32[24,768]{1,0:T(8,128)S(1)} %add_rsqrt_fusion.1, f32[24,768]{1,0:T(8,128)S(1)} %broadcast_multiply_fusion.1), kind=kOutput, calls=%fused_computation.144 | convolution fusion | flops 2448949248 | bytes 28591104 | tf_op jit(solution)/shard_map/dot_general | solution.py:104
  101.4 365.5 %all-to-all-done = bf16[2,1,24,768,256]{4,3,2,1,0:T(8,128)(2,1)} async-done(((bf16[2,1,24,768,256]{4,3,2,1,0:T(8,128)(2,1)}), bf16[2,1,24,768,256]{4,3,2,1,0:T(8,128)(2,1)}, u32[]{:S(2)}, u32[]{:S(2)}) %all-to-all-start) | async-done | bytes 18874400 | tf_op jit(solution)/shard_map/all_to_all | solution.py:115
  466.9 24.4 %copy.206 = bf16[2,1,24,768,256]{3,4,2,0,1:T(8,128)(2,1)} copy(bf16[2,1,24,768,256]{4,3,2,1,0:T(8,128)(2,1)} %all-to-all-done) | data formatting | bytes 37748736
  491.4 24.7 %copy.207 = bf16[48,768,256]{1,2,0:T(8,128)(2,1)} copy(bf16[48,768,256]{2,1,0:T(8,128)(2,1)} %all-gather.3.cloned.1.call-done) | data formatting | bytes 37748736
  516.1 19.4 %multiply_reduce_fusion.1 = f32[24,8,768,2]{2,1,0,3:T(8,128)S(1)} fusion(bf16[24,8,768,32,2]{2,3,1,0,4:T(8,128)(2,1)} %bitcast.175, f32[24,8,768,32]{2,3,1,0:T(8,128)} %bitcast_convert_fusion.3), kind=kLoop, calls=%fused_computation.1 | loop fusion | flops 28016640 | bytes 38928384
  536.0 15.3 %multiply_reduce_fusion = f32[24,768,8,32]{1,3,2,0:T(8,128)} fusion(bf16[24,768,8,2,32]{1,4,2,0,3:T(8,128)(2,1)S(1)} %bitcast.174, f32[24,768,8,2]{1,2,3,0:T(8,128)S(1)} %get-tuple-element.6), kind=kLoop, calls=%fused_computation | loop fusion | flops 23592960 | bytes 38928384 | tf_op jit(solution)/shard_map/nmlhw,nlwhe->mlwhe/dot_general | solution.py:88
  551.3 11.9 divide_convert_fusion
  563.2 20.6 %convert_reduce_fusion = (f32[24,768]{1,0:T(8,128)S(1)}, bf16[1,24,768,256]{2,3,1,0:T(8,128)(2,1)}) fusion(bf16[24,768,256]{1,2,0:T(8,128)(2,1)} %bitcast.176, bf16[256,256]{1,0:T(8,128)(2,1)S(1)} %copy-done, bf16[1,24,768,256]{2,3,1,0:T(8,128)(2,1)} %copy.142), kind=kOutput, calls=%fused_computation.4 | convolution fusion | flops 2439493632 | bytes 28516352 | tf_op jit(solution)/shard_map/dot_general | solution.py:118
  590.2 10.8 fusion.15
  608.6 39.1 %copy.160 = bf16[1,24,2,384,256]{4,2,1,0,3:T(2,128)(2,1)} copy(bf16[1,24,2,384,256]{4,3,2,1,0:T(8,128)(2,1)S(1)} %multiply_convert_fusion) | data formatting | bytes 18874368 | tf_op jit(solution)/shard_map/convert_element_type | solution.py:128
  656.5 202.5 %all-to-all-done.1 = bf16[1,24,2,384,256]{4,2,1,0,3:T(2,128)(2,1)} async-done(((bf16[1,24,2,384,256]{4,2,1,0,3:T(2,128)(2,1)}), bf16[1,24,2,384,256]{4,2,1,0,3:T(2,128)(2,1)}, u32[]{:S(2)}, u32[]{:S(2)}) %all-to-all-start.1) | async-done | bytes 9437216 | tf_op jit(solution)/shard_map/all_to_all | solution.py:136
  859.1 10.8 copy.161
  878.1 19.5 %bitcast_convert_fusion.2 = bf16[24,256,2,128]{3,1,2,0:T(8,128)(2,1)S(1)} fusion(bf16[384,2,24,256,1]{3,2,1,0,4:T(8,128)(2,1)} %bitcast.182, bf16[1,128,2,384]{3,1,2,0:T(8,128)(2,1)S(1)} %get-tuple-element.14, bf16[1,128,2,384]{3,1,2,0:T(8,128)(2,1)S(1)} %get-tuple-element.13), kind=kOutput, calls=%fused_computation.41 | convolution fusion | flops 2418278400 | bytes 12976128 | tf_op jit(solution)/shard_map/pqrj,mjrkd->mpqkd/dot_general | solution.py:133
  905.7 24.0 %copy.168 = bf16[1,384,2,24,256]{4,2,3,0,1:T(2,128)(2,1)} copy(bf16[1,384,2,24,256]{1,4,2,3,0:T(8,128)(2,1)} %fusion.12) | data formatting | bytes 18874368 | tf_op jit(solution)/shard_map/convert_element_type | solution.py:143
  940.0 199.5 %all-to-all-done.2 = bf16[1,384,2,24,256]{4,2,3,0,1:T(2,128)(2,1)} async-done(((bf16[1,384,2,24,256]{4,2,3,0,1:T(2,128)(2,1)}), bf16[1,384,2,24,256]{4,2,3,0,1:T(2,128)(2,1)}, u32[]{:S(2)}, u32[]{:S(2)}) %all-to-all-start.2) | async-done | bytes 9437216 | tf_op jit(solution)/shard_map/all_to_all | solution.py:144
  1139.5 9.0 copy.169
  1148.5 8.6 copy.170
  1157.1 15.6 %fusion.11 = bf16[1,24,768,256]{2,3,1,0:T(8,128)(2,1)} fusion(bf16[1,24,768,256]{2,3,1,0:T(8,128)(2,1)} %get-tuple-element.26, bf16[24,2,384,256]{3,2,1,0:T(8,128)(2,1)} %bitcast.181, bf16[24,384]{1,0:T(8,128)(2,1)S(1)} %copy-done.7, bf16[1,384,768]{1,2,0:T(8,128)(2,1)S(1)} %get-tuple-element.16, bf16[1,384,768]{1,2,0:T(8,128)(2,1)S(1)} %get-tuple-element.15), kind=kOutput, calls=%fused_computation.19 | convolution fusion | flops 7283146752 | bytes 29509632 | tf_op jit(solution)/shard_map/mjrkd,rkx->mjxd/dot_general | solution.py:146
  1172.7 12.6 %copy.172 = bf16[1,24,768,256]{3,2,1,0:T(8,128)(2,1)} copy(bf16[1,24,768,256]{2,3,1,0:T(8,128)(2,1)} %fusion.11) | data formatting | bytes 18874368 | tf_op jit(solution)/shard_map/convert_element_type | solution.py:152
  (72 shorter events, 65.3 us)
Async XLA Ops:
  6.5 556.6 %copy-start = (bf16[256,256]{1,0:T(8,128)(2,1)S(1)}, bf16[256,256]{1,0:T(8,128)(2,1)}, u32[]{:S(2)}) copy-start(bf16[256,256]{1,0:T(8,128)(2,1)} %param.16) | copy-start | bytes 393220
  6.5 484.9 %all-gather.3.cloned.1.call-start = ((), (), s32[]{:S(2)}) async-start(), calls=%async_computation.3 | async-start | bytes 28311552 | tf_op jit(solution)/shard_map/all_gather | solution.py:108
  19.2 6.4 copy-start.2
  19.2 9.0 copy-start.8
  19.2 9.0 copy-start.10
  39.2 0.9 copy-start.11
  71.7 15.9 %copy-start.9 = (s32[24]{0:T(128)S(1)}, s32[24]{0:T(128)}, u32[]{:S(2)}) copy-start(s32[24]{0:T(128)} %param.11) | copy-start | bytes 292
  71.7 16.6 %copy-start.4 = (bf16[256,256]{1,0:T(8,128)(2,1)S(1)}, bf16[256,256]{1,0:T(8,128)(2,1)}, u32[]{:S(2)}) copy-start(bf16[256,256]{1,0:T(8,128)(2,1)} %param.13) | copy-start | bytes 393220
  71.7 395.3 %all-to-all-start = ((bf16[2,1,24,768,256]{4,3,2,1,0:T(8,128)(2,1)}), bf16[2,1,24,768,256]{4,3,2,1,0:T(8,128)(2,1)}, u32[]{:S(2)}, u32[]{:S(2)}) async-start(bf16[2,1,24,768,256]{4,3,2,1,0:T(8,128)(2,1)} %pad_maximum_fusion), calls=%async_computation | async-start | bytes 37748736 | tf_op jit(solution)/shard_map/all_to_all | solution.py:115
  516.1 19.8 %slice-start = ((s8[18874368]{0:T(1024)(128)(4,1)}), s8[4194304]{0:T(1024)(128)(4,1)S(1)}, s32[]{:S(2)}) async-start(s8[18874368]{0:T(1024)(128)(4,1)} %bitcast.172), calls=%async_computation.4 | async-start | bytes 8388608
  516.1 19.8 %slice-start.1 = ((s8[18874368]{0:T(1024)(128)(4,1)}), s8[4194304]{0:T(1024)(128)(4,1)S(1)}, s32[]{:S(2)}) async-start(s8[18874368]{0:T(1024)(128)(4,1)} %bitcast.172), calls=%async_computation.5 | async-start | bytes 8388608
  516.1 19.8 %slice-start.2 = ((s8[18874368]{0:T(1024)(128)(4,1)}), s8[4194304]{0:T(1024)(128)(4,1)S(1)}, s32[]{:S(2)}) async-start(s8[18874368]{0:T(1024)(128)(4,1)} %bitcast.172), calls=%async_computation.6 | async-start | bytes 8388608
  516.1 19.8 %slice-start.3 = ((s8[18874368]{0:T(1024)(128)(4,1)}), s8[4194304]{0:T(1024)(128)(4,1)S(1)}, s32[]{:S(2)}) async-start(s8[18874368]{0:T(1024)(128)(4,1)} %bitcast.172), calls=%async_computation.7 | async-start | bytes 8388608
  516.1 19.8 %slice-start.4 = ((s8[18874368]{0:T(1024)(128)(4,1)}), s8[2097152]{0:T(1024)(128)(4,1)S(1)}, s32[]{:S(2)}) async-start(s8[18874368]{0:T(1024)(128)(4,1)} %bitcast.172), calls=%async_computation.8 | async-start | bytes 4194304
  583.7 6.5 copy-start.3
  583.7 6.5 copy-start.12
  647.7 6.5 copy-start.5
  647.7 6.7 copy-start.6
  647.7 211.3 %all-to-all-start.1 = ((bf16[1,24,2,384,256]{4,2,1,0,3:T(2,128)(2,1)}), bf16[1,24,2,384,256]{4,2,1,0,3:T(2,128)(2,1)}, u32[]{:S(2)}, u32[]{:S(2)}) async-start(bf16[1,24,2,384,256]{4,2,1,0,3:T(2,128)(2,1)} %copy.160), calls=%async_computation.1 | async-start | bytes 18874368 | tf_op jit(solution)/shard_map/all_to_all | solution.py:136
  929.7 209.9 %all-to-all-start.2 = ((bf16[1,384,2,24,256]{4,2,3,0,1:T(2,128)(2,1)}), bf16[1,384,2,24,256]{4,2,3,0,1:T(2,128)(2,1)}, u32[]{:S(2)}, u32[]{:S(2)}) async-start(bf16[1,384,2,24,256]{4,2,3,0,1:T(2,128)(2,1)} %copy.168), calls=%async_computation.2 | async-start | bytes 18874368 | tf_op jit(solution)/shard_map/all_to_all | solution.py:144
  1148.5 8.6 copy-start.7
  1157.1 28.2 %copy-start.1 = (bf16[256,256]{1,0:T(8,128)(2,1)S(1)}, bf16[256,256]{1,0:T(8,128)(2,1)}, u32[]{:S(2)}) copy-start(bf16[256,256]{1,0:T(8,128)(2,1)} %param.16) | copy-start | bytes 393220
Sparse Core Ops, SparseCore 0:
  39.4 403.9 all-gather.2
